TPU v7x, 32 devices: a whole 2x2x4 slice. The times are simulated.
32 devices in a mesh: rows: 16 (over z, x, core), cols: 2 (over y).
Axes of the slice: x: 2, y: 2, z: 4, core: 2. Of those that a mesh axis runs over, the one named last changes fastest.
Arguments:
- states: float32 [32, 16384], P('cols', 'rows'), may hold values from -120 to 120, as said below
- adj_weight: bfloat16 [128, 3, 128, 128], P('rows'), may hold values from 0.099609375 to 2
- adj_index: int32 [128, 3], P('rows'), may hold values from 0 to 127, as said below
- partner: int32 [128], P('rows'), may hold values from 0 to 127, as said below
Outputs:
- correction: float32 [32, 16384], P('cols', 'rows')
Inputs may be any that keep to these rules, and one draw needn't show every extreme that they name: adj_index[b, 0] = b; every other entry lies within 4 blocks of b. partner[partner[b]] = b and partner[b] != b; the 8 blocks of one index of rows have their partners on 8 different other indices of rows, at most one block on each. `states`: finite values.
All inputs are finite; a program needn't handle non-finite values.
Results may differ from a plain program's by a relative error of at most 0.0003.
Values sent between devices are 32-bit elements; how exact they have to be, the bound alone decides.
No kernel may reach another device: no remote copies, remote signals or barrier semaphores. Data moves between devices by JAX's collectives and lax.ppermute only.
A program may use at most 64 MiB of HBM per device.

v0:
```python
import jax
import jax.numpy as jnp
from jax import lax
from jax.sharding import PartitionSpec as P

DAMPING = 2.0 / 3.0
EPSILON = 1e-06
EXACT = lax.Precision.HIGHEST


def extended(shard, sides, width):
    for axis, dim in sides:
        peers, length = (lax.axis_size(axis), shard.shape[dim])
        up = [(i, (i + 1) % peers) for i in range(peers - 1)]
        down = [(j, i) for i, j in up]
        last = lax.slice_in_dim(shard, length - width, length, axis=dim)
        initial = lax.slice_in_dim(shard, 0, width, axis=dim)
        before = lax.ppermute(last, axis, up)
        after = lax.ppermute(initial, axis, down)
        shard = jnp.concatenate([before, shard, after], axis=dim)
    return shard


def to_slots(values, owner_dev, row_devices):
    empty = jnp.zeros((values.shape[0], row_devices, values.shape[2]), values.dtype)
    return empty.at[:, owner_dev].set(values)


def from_slots(arrived, owner_dev):
    return arrived[:, owner_dev]


def solve_ritz(gram_matrix, rayleigh):
    factor = jnp.linalg.cholesky(gram_matrix)
    return jax.scipy.linalg.cho_solve((factor, True), rayleigh)


def local(states, adj_weight, adj_index, partner):
    local_cols, vertices = states.shape
    blocks_here = adj_weight.shape[0]
    block_len = adj_weight.shape[2]
    row_devices = lax.axis_size("rows")
    margin_blocks = blocks_here // 2
    local_ids = adj_index - (lax.axis_index("rows") * blocks_here - margin_blocks)
    owner_dev = partner // blocks_here
    degree = jnp.sum(adj_weight, axis=(1, 3), dtype=jnp.float32).reshape(vertices)
    degree_blocks = degree.reshape(1, blocks_here, block_len)

    def operate(vector_in):
        widened = extended(vector_in, (("rows", 1),), margin_blocks * block_len)
        grid_blocks = widened.reshape(local_cols, -1, block_len)
        picked = grid_blocks[:, local_ids]
        neighbour = jnp.einsum(
            "bkij,cbkj->cbi",
            adj_weight,
            picked,
            precision=EXACT,
            preferred_element_type=jnp.float32,
        )
        return degree * vector_in - neighbour.reshape(local_cols, vertices)

    applied = operate(states)
    all_states = lax.all_gather(states, "cols", axis=0, tiled=True)
    gram_part = jnp.einsum("cv,dv->cd", all_states * degree, all_states, precision=EXACT)
    rayleigh_part = jnp.einsum("cv,dv->cd", all_states, applied, precision=EXACT)
    gram_matrix, rayleigh = lax.psum((gram_part, rayleigh_part), "rows")
    ritz_matrix = solve_ritz(gram_matrix, rayleigh)
    residual = applied - degree * jnp.einsum("cd,cv->dv", ritz_matrix, all_states, precision=EXACT)
    presmooth = DAMPING * residual / degree
    remain = (residual - operate(presmooth)).reshape(local_cols, blocks_here, block_len)
    arrived, arrived_degree = (
        lax.all_to_all(
            to_slots(remain, owner_dev, row_devices),
            "rows",
            split_axis=1,
            concat_axis=1,
            tiled=True,
        ),
        lax.all_to_all(
            to_slots(degree_blocks, owner_dev, row_devices),
            "rows",
            split_axis=1,
            concat_axis=1,
            tiled=True,
        ),
    )
    coarse_degree = (degree_blocks + from_slots(arrived_degree, owner_dev)).reshape(vertices)
    coarse = (remain + from_slots(arrived, owner_dev)).reshape(local_cols, vertices)
    coarse_fix = DAMPING * coarse / coarse_degree
    product = operate(coarse_fix).reshape(local_cols, blocks_here, block_len)
    arrived_product = lax.all_to_all(
        to_slots(product, owner_dev, row_devices), "rows", split_axis=1, concat_axis=1, tiled=True
    )
    coarse_image = (product + from_slots(arrived_product, owner_dev)).reshape(local_cols, vertices)
    coarse_fix = coarse_fix + DAMPING * (coarse - coarse_image) / coarse_degree
    second = presmooth + coarse_fix
    smooth = second + DAMPING * (residual - operate(second)) / degree
    squares = lax.psum(jnp.sum(smooth * smooth, axis=1), "rows")
    return smooth / jnp.sqrt(squares / (vertices * row_devices) + EPSILON)[:, None]


def solution(mesh):
    return jax.shard_map(
        local,
        mesh=mesh,
        in_specs=(P("cols", "rows"), P("rows", None, None, None), P("rows", None), P("rows")),
        out_specs=P("cols", "rows"),
        check_vma=False,
    )
```

profile of v0, /device:TPU:0, one launch (start us, length us, event | category | flops | bytes accessed | tf_op | source)
XLA Modules:
  0.0 170.4 jit_solution(17137495620325622604)
XLA Ops:
  0.8 2.4 %collective-permute-start = (f32[16,512]{1,0:T(8,128)S(1)}, f32[16,512]{1,0:T(8,128)S(1)}, u32[]{:S(2)}, u32[]{:S(2)}) collective-permute-start(f32[16,512]{1,0:T(8,128)S(1)} %get-tuple-element.15), channel_id=1, source_target_pairs={{0,2},{2,4},{4,6},{6,8},{8,10},{10,12},{12,14},{14,16},{16,18},{18... | collective-permute-start | bytes 98312 | tf_op jit(solution)/shard_map/ppermute | solution.py:18
  3.2 1.3 collective-permute-start.1
  4.5 5.5 %all_gather.3 = f32[32,1024]{1,0:T(8,128)S(1)} all-gather(f32[16,1024]{1,0:T(8,128)} %param.4), channel_id=1, replica_groups=mesh['rows'=16,'cols'=2] {'cols'}, dimensions={0}, use_global_device_ids=true | all-gather | bytes 196608 | tf_op jit(solution)/shard_map/all_gather | solution.py:63
  10.9 1.4 convert_reduce_fusion
  13.3 0.9 convolution_bitcast_fusion.3
  14.4 62.2 %all-reduce = (f32[32,16]{0,1:T(8,128)S(1)}, f32[32,32]{0,1:T(8,128)S(1)}) all-reduce(f32[32,16]{0,1:T(8,128)S(1)} %convolution_bitcast_fusion.4, f32[32,32]{0,1:T(8,128)S(1)} %fusion.1), channel_id=1, replica_groups=mesh['rows'=16,'cols'=2] {'rows'}, use_global_device_ids=true, to_apply=%region_4.5 | all-reduce | flops 1536 | bytes 12288 | tf_op jit(solution)/shard_map/psum | solution.py:66
  76.7 2.9 %cholesky.16 = f32[32,32]{1,0:T(8,128)S(1)} custom-call(f32[32,32]{1,0:T(8,128)S(1)} %fusion.20), custom_call_target="Cholesky" | custom-call | tf_op jit(solution)/shard_map/jit(cholesky)/cholesky | solution.py:34
  81.0 2.4 %custom-call.10 = f32[1,32,32]{1,2,0:T(8,128)S(1)} custom-call(f32[1,32,32]{2,1,0:T(8,128)S(1)} %fusion.15), custom_call_target="InvertDiagBlocksLowerTriangular" | custom-call | tf_op jit(solution)/shard_map/jit(_cho_solve)/triangular_solve | solution.py:35
  83.9 1.3 collective-permute-start.2
  85.2 1.3 collective-permute-start.3
  86.6 1.2 scatter_custom_fusion.1
  87.7 3.5 %all-to-all-start.1 = ((f32[1,16,128]{2,0,1:T(1,128)}), f32[1,16,128]{2,0,1:T(1,128)S(1)}, u32[]{:S(2)}, u32[]{:S(2)}) async-start(f32[1,16,128]{2,0,1:T(1,128)} %bitcast.17), calls=%async_computation.1 | async-start | bytes 16384 | tf_op jit(solution)/shard_map/all_to_all | solution.py:79
  93.4 2.0 %scatter_fusion = f32[16,16,128]{2,0,1:T(8,128)} fusion(f32[16,16,128]{2,0,1:T(8,128)} %broadcast.109.clone, s32[8]{0:T(128)S(1)} %compare_select_fusion.1, f32[8,16,128]{2,1,0:T(8,128)S(1)} %bitcast_bitcast_fusion.1), kind=kCustom, calls=%fused_computation.7 | custom fusion | bytes 196640 | tf_op jit(solution)/shard_map/scatter | solution.py:26
  95.4 2.1 %all-to-all-done.1 = f32[1,16,128]{2,0,1:T(1,128)S(1)} async-done(((f32[1,16,128]{2,0,1:T(1,128)}), f32[1,16,128]{2,0,1:T(1,128)S(1)}, u32[]{:S(2)}, u32[]{:S(2)}) %all-to-all-start.1) | async-done | bytes 8224 | tf_op jit(solution)/shard_map/all_to_all | solution.py:79
  97.5 3.9 %all-to-all-start = ((f32[16,16,128]{2,0,1:T(8,128)}), f32[16,16,128]{2,0,1:T(8,128)S(1)}, u32[]{:S(2)}, u32[]{:S(2)}) async-start(f32[16,16,128]{2,0,1:T(8,128)} %scatter_fusion), calls=%async_computation | async-start | bytes 262144 | tf_op jit(solution)/shard_map/all_to_all | solution.py:72
  102.0 7.3 %all-to-all-done = f32[16,16,128]{2,0,1:T(8,128)S(1)} async-done(((f32[16,16,128]{2,0,1:T(8,128)}), f32[16,16,128]{2,0,1:T(8,128)S(1)}, u32[]{:S(2)}, u32[]{:S(2)}) %all-to-all-start) | async-done | bytes 131104 | tf_op jit(solution)/shard_map/all_to_all | solution.py:72
  109.9 1.3 collective-permute-start.4
  111.2 1.3 collective-permute-start.5
  112.5 1.8 %collective-permute-done.5 = f32[16,512]{1,0:T(8,128)S(1)} collective-permute-done((f32[16,512]{1,0:T(8,128)S(1)}, f32[16,512]{1,0:T(8,128)S(1)}, u32[]{:S(2)}, u32[]{:S(2)}) %collective-permute-start.5) | collective-permute-done | bytes 32800 | tf_op jit(solution)/shard_map/ppermute | solution.py:19
  116.6 14.6 %all_to_all.15 = f32[16,16,128]{2,0,1:T(8,128)S(1)} all-to-all(f32[16,16,128]{2,0,1:T(8,128)S(1)} %scatter_fusion.1), channel_id=1, replica_groups=mesh['rows'=16,'cols'=2] {'rows'}, dimensions={1} | all-to-all | bytes 262144 | tf_op jit(solution)/shard_map/all_to_all | solution.py:91
  131.9 1.3 collective-permute-start.6
  133.2 1.3 collective-permute-start.7
  134.5 1.8 %collective-permute-done.7 = f32[16,512]{1,0:T(8,128)S(1)} collective-permute-done((f32[16,512]{1,0:T(8,128)S(1)}, f32[16,512]{1,0:T(8,128)S(1)}, u32[]{:S(2)}, u32[]{:S(2)}) %collective-permute-start.7) | collective-permute-done | bytes 32800 | tf_op jit(solution)/shard_map/ppermute | solution.py:19
  137.9 31.7 %psum.23 = f32[16]{0:T(128)S(1)} all-reduce(f32[16]{0:T(128)S(1)} %get-tuple-element.7), channel_id=1, replica_groups=mesh['rows'=16,'cols'=2] {'rows'}, use_global_device_ids=true, to_apply=%region_9.10 | all-reduce | flops 16 | bytes 128 | tf_op jit(solution)/shard_map/psum | solution.py:98
  (57 shorter events, 13.3 us)
Async XLA Ops:
  0.0 12.6 %copy-start.1 = (f32[16,1024]{1,0:T(8,128)S(1)}, f32[16,1024]{1,0:T(8,128)}, u32[]{:S(2)}) copy-start(f32[16,1024]{1,0:T(8,128)} %param.4) | copy-start | bytes 196612
  0.8 11.8 %collective-permute-start = (f32[16,512]{1,0:T(8,128)S(1)}, f32[16,512]{1,0:T(8,128)S(1)}, u32[]{:S(2)}, u32[]{:S(2)}) collective-permute-start(f32[16,512]{1,0:T(8,128)S(1)} %get-tuple-element.15), channel_id=1, source_target_pairs={{0,2},{2,4},{4,6},{6,8},{8,10},{10,12},{12,14},{14,16},{16,18},{18... | collective-permute-start | bytes 98312 | tf_op jit(solution)/shard_map/ppermute | solution.py:18
  3.2 9.4 %collective-permute-start.1 = (f32[16,512]{1,0:T(8,128)S(1)}, f32[16,512]{1,0:T(8,128)S(1)}, u32[]{:S(2)}, u32[]{:S(2)}) collective-permute-start(f32[16,512]{1,0:T(8,128)S(1)} %get-tuple-element.16), channel_id=1, source_target_pairs={{2,0},{4,2},{6,4},{8,6},{10,8},{12,10},{14,12},{16,14},{18,16},{20... | collective-permute-start | bytes 98312 | tf_op jit(solution)/shard_map/ppermute | solution.py:19
  10.9 2.3 %copy-start = (bf16[8,3,128,128]{3,2,1,0:T(8,128)(2,1)S(1)}, bf16[8,3,128,128]{3,2,1,0:T(8,128)(2,1)}, u32[]{:S(2)}) copy-start(bf16[8,3,128,128]{3,2,1,0:T(8,128)(2,1)} %param.5) | copy-start | bytes 2359300
  14.2 72.4 %copy-start.2 = (s32[8]{0:T(128)S(1)}, s32[8]{0:T(128)}, u32[]{:S(2)}) copy-start(s32[8]{0:T(128)} %param.7) | copy-start | bytes 100
  83.9 7.3 %collective-permute-start.2 = (f32[16,512]{1,0:T(8,128)S(1)}, f32[16,512]{1,0:T(8,128)S(1)}, u32[]{:S(2)}, u32[]{:S(2)}) collective-permute-start(f32[16,512]{1,0:T(8,128)S(1)} %get-tuple-element.13), channel_id=1, source_target_pairs={{0,2},{2,4},{4,6},{6,8},{8,10},{10,12},{12,14},{14,16},{16,18},{18... | collective-permute-start | bytes 98312 | tf_op jit(solution)/shard_map/ppermute | solution.py:18
  85.2 6.0 %collective-permute-start.3 = (f32[16,512]{1,0:T(8,128)S(1)}, f32[16,512]{1,0:T(8,128)S(1)}, u32[]{:S(2)}, u32[]{:S(2)}) collective-permute-start(f32[16,512]{1,0:T(8,128)S(1)} %get-tuple-element.14), channel_id=1, source_target_pairs={{2,0},{4,2},{6,4},{8,6},{10,8},{12,10},{14,12},{16,14},{18,16},{20... | collective-permute-start | bytes 98312 | tf_op jit(solution)/shard_map/ppermute | solution.py:19
  87.7 9.8 %all-to-all-start.1 = ((f32[1,16,128]{2,0,1:T(1,128)}), f32[1,16,128]{2,0,1:T(1,128)S(1)}, u32[]{:S(2)}, u32[]{:S(2)}) async-start(f32[1,16,128]{2,0,1:T(1,128)} %bitcast.17), calls=%async_computation.1 | async-start | bytes 16384 | tf_op jit(solution)/shard_map/all_to_all | solution.py:79
  97.5 11.8 %all-to-all-start = ((f32[16,16,128]{2,0,1:T(8,128)}), f32[16,16,128]{2,0,1:T(8,128)S(1)}, u32[]{:S(2)}, u32[]{:S(2)}) async-start(f32[16,16,128]{2,0,1:T(8,128)} %scatter_fusion), calls=%async_computation | async-start | bytes 262144 | tf_op jit(solution)/shard_map/all_to_all | solution.py:72
  109.9 2.6 %collective-permute-start.4 = (f32[16,512]{1,0:T(8,128)S(1)}, f32[16,512]{1,0:T(8,128)S(1)}, u32[]{:S(2)}, u32[]{:S(2)}) collective-permute-start(f32[16,512]{1,0:T(8,128)S(1)} %get-tuple-element.11), channel_id=1, source_target_pairs={{0,2},{2,4},{4,6},{6,8},{8,10},{10,12},{12,14},{14,16},{16,18},{18... | collective-permute-start | bytes 98312 | tf_op jit(solution)/shard_map/ppermute | solution.py:18
  111.2 3.1 %collective-permute-start.5 = (f32[16,512]{1,0:T(8,128)S(1)}, f32[16,512]{1,0:T(8,128)S(1)}, u32[]{:S(2)}, u32[]{:S(2)}) collective-permute-start(f32[16,512]{1,0:T(8,128)S(1)} %get-tuple-element.12), channel_id=1, source_target_pairs={{2,0},{4,2},{6,4},{8,6},{10,8},{12,10},{14,12},{16,14},{18,16},{20... | collective-permute-start | bytes 98312 | tf_op jit(solution)/shard_map/ppermute | solution.py:19
  131.9 2.6 %collective-permute-start.6 = (f32[16,512]{1,0:T(8,128)S(1)}, f32[16,512]{1,0:T(8,128)S(1)}, u32[]{:S(2)}, u32[]{:S(2)}) collective-permute-start(f32[16,512]{1,0:T(8,128)S(1)} %get-tuple-element.9), channel_id=1, source_target_pairs={{0,2},{2,4},{4,6},{6,8},{8,10},{10,12},{12,14},{14,16},{16,18},{18... | collective-permute-start | bytes 98312 | tf_op jit(solution)/shard_map/ppermute | solution.py:18
  133.2 3.1 %collective-permute-start.7 = (f32[16,512]{1,0:T(8,128)S(1)}, f32[16,512]{1,0:T(8,128)S(1)}, u32[]{:S(2)}, u32[]{:S(2)}) collective-permute-start(f32[16,512]{1,0:T(8,128)S(1)} %get-tuple-element.10), channel_id=1, source_target_pairs={{2,0},{4,2},{6,4},{8,6},{10,8},{12,10},{14,12},{16,14},{18,16},{20... | collective-permute-start | bytes 98312 | tf_op jit(solution)/shard_map/ppermute | solution.py:19
where the time goes:
time: 171 us; the launch traced here: 170 us
  blocking collectives  114 us (67%)
  starting transfers between devices  18.8 us (11%)
  waiting for transfers between devices  13 us (8%)
  other arithmetic  9.87 us (6%)
  local copies, waits for them, and re-layouts  9.62 us (6%)
  matrix products  4.63 us (3%)
    psum x1, blocking collectives, local(): gram_matrix, rayleigh = lax.psum((gram_part, rayleigh_part), 'rows')  62.2 us
    psum x1, blocking collectives, local(): squares = lax.psum(jnp.sum(smooth * smooth, axis=1), 'rows')  31.7 us
    all_to_all x1, blocking collectives, local(): lax.all_to_all(to_slots(product, owner_dev, row_devices), 'rows', split_a...  14.6 us
    all_to_all x1, waiting for transfers between devices, local(): lax.all_to_all(to_slots(remain, owner_dev, row_devices), 'rows', split_ax...  7.32 us
    ppermute x4, starting transfers between devices, extended(): before = lax.ppermute(last, axis, up)  6.26 us
    all_gather x1, blocking collectives, local(): all_states = lax.all_gather(states, 'cols', axis=0, tiled=True)  5.51 us
    ppermute x4, starting transfers between devices, extended(): after = lax.ppermute(initial, axis, down)  5.17 us
    scatter x3, local copies, waits for them, and re-layouts, to_slots(): return empty.at[:, owner_dev].set(values)  3.89 us
  transfers between devices with their start and end apart: 10, of which 4 were waited for; matrix products, arithmetic and copies ran while one was open for 5% of the time, Pallas kernels for 0%

commit v1 on v0

--- a/solution.py
+++ b/solution.py
@@ -6,6 +6,25 @@
 DAMPING = 2.0 / 3.0
 EPSILON = 1e-06
 EXACT = lax.Precision.HIGHEST
+
+
+def direct_cubes(a0, along_axis):
+    field_out = lax.axis_size(along_axis)
+    low = lax.axis_index(along_axis)
+    x_now, u_next = (field_out, low)
+    extra = a0.shape[1] // x_now
+    work_now = jnp.roll(a0, -u_next * extra, 1)
+    opened = lax.slice_in_dim(work_now, 0, extra, axis=1)
+    line_up = [opened]
+    for q in [*range(1, x_now)]:
+        u1 = lax.slice_in_dim(work_now, q * extra, (q + 1) * extra, axis=1)
+        back = lax.ppermute(
+            u1, axis_name=along_axis, perm=[(k, (k + q) % x_now) for k in range(x_now)]
+        )
+        line_up.append(back)
+    v_next = jnp.concatenate(line_up[::-1], 1)
+    local_out = jnp.roll(v_next, (u_next + 1) * line_up[0].shape[1], 1)
+    return local_out
 
 
 def extended(shard, sides, width):
@@ -88,9 +107,7 @@
     coarse = (remain + from_slots(arrived, owner_dev)).reshape(local_cols, vertices)
     coarse_fix = DAMPING * coarse / coarse_degree
     product = operate(coarse_fix).reshape(local_cols, blocks_here, block_len)
-    arrived_product = lax.all_to_all(
-        to_slots(product, owner_dev, row_devices), "rows", split_axis=1, concat_axis=1, tiled=True
-    )
+    arrived_product = direct_cubes(to_slots(product, owner_dev, row_devices), along_axis="rows")
     coarse_image = (product + from_slots(arrived_product, owner_dev)).reshape(local_cols, vertices)
     coarse_fix = coarse_fix + DAMPING * (coarse - coarse_image) / coarse_degree
     second = presmooth + coarse_fix

time: 171 us -> 218 us (1.27)
  starting transfers between devices: 18.8 us -> 59.6 us
  waiting for transfers between devices: 13 us -> 33.4 us
  blocking collectives: 114 us -> 99.9 us
    ppermute x0 -> x15, starting transfers between devices: none -> 40.8 us  [direct_cubes(): lax.ppermute(u1, axis_name=along_axis, perm=[(k, (k + q) % x_now) for k i...]
    ppermute x0 -> x15, waiting for transfers between devices: none -> 17.3 us  [direct_cubes(): lax.ppermute(u1, axis_name=along_axis, perm=[(k, (k + q) % x_now) for k i...]
    all_to_all x1 -> x0, blocking collectives: 14.6 us -> none  [local(): lax.all_to_all(to_slots(product, owner_dev, row_devices), 'rows', split_a...]
    ppermute x4, waiting for transfers between devices: 3.59 us -> 6.72 us  [extended(): after = lax.ppermute(initial, axis, down)]
  transfers between devices with their start and end apart: 10 -> 25, of which waited for: 4 -> 14; matrix products, arithmetic and copies ran while one was open for 5% -> 4% of each run, Pallas kernels for 0% -> 0%
where the time goes in v1:
time: 218 us
  blocking collectives  99.9 us (46%)
  starting transfers between devices  59.6 us (27%)
  waiting for transfers between devices  33.4 us (15%)
  other arithmetic  9.98 us (5%)
  local copies, waits for them, and re-layouts  9.68 us (4%)
  matrix products  4.63 us (2%)
    psum x1, blocking collectives, local(): gram_matrix, rayleigh = lax.psum((gram_part, rayleigh_part), 'rows')  62.2 us
    ppermute x15, starting transfers between devices, direct_cubes(): lax.ppermute(u1, axis_name=along_axis, perm=[(k, (k + q) % x_now) for k i...  40.8 us
    psum x1, blocking collectives, local(): squares = lax.psum(jnp.sum(smooth * smooth, axis=1), 'rows')  32.1 us
    ppermute x15, waiting for transfers between devices, direct_cubes(): lax.ppermute(u1, axis_name=along_axis, perm=[(k, (k + q) % x_now) for k i...  17.3 us
    all_to_all x1, waiting for transfers between devices, local(): lax.all_to_all(to_slots(remain, owner_dev, row_devices), 'rows', split_ax...  7.32 us
    ppermute x4, waiting for transfers between devices, extended(): after = lax.ppermute(initial, axis, down)  6.72 us
    ppermute x4, starting transfers between devices, extended(): before = lax.ppermute(last, axis, up)  6.26 us
    all_gather x1, blocking collectives, local(): all_states = lax.all_gather(states, 'cols', axis=0, tiled=True)  5.51 us
  transfers between devices with their start and end apart: 25, of which 14 were waited for; matrix products, arithmetic and copies ran while one was open for 4% of the time, Pallas kernels for 0%

profile of v1, /device:TPU:0, one launch (start us, length us, event | category | flops | bytes accessed | tf_op | source)
XLA Modules:
  0.0 217.7 jit_solution(16097915560305221612)
XLA Ops:
  0.8 2.4 %collective-permute-start = (f32[16,512]{1,0:T(8,128)S(1)}, f32[16,512]{1,0:T(8,128)S(1)}, u32[]{:S(2)}, u32[]{:S(2)}) collective-permute-start(f32[16,512]{1,0:T(8,128)S(1)} %get-tuple-element.31), channel_id=1, source_target_pairs={{0,2},{2,4},{4,6},{6,8},{8,10},{10,12},{12,14},{14,16},{16,18},{18... | collective-permute-start | bytes 98312 | tf_op jit(solution)/shard_map/ppermute | solution.py:37
  4.5 5.5 %all_gather.3 = f32[32,1024]{1,0:T(8,128)S(1)} all-gather(f32[16,1024]{1,0:T(8,128)} %param.6), channel_id=1, replica_groups=mesh['rows'=16,'cols'=2] {'cols'}, dimensions={0}, use_global_device_ids=true | all-gather | bytes 196608 | tf_op jit(solution)/shard_map/all_gather | solution.py:82
  14.4 62.2 %all-reduce = (f32[32,16]{0,1:T(8,128)S(1)}, f32[32,32]{0,1:T(8,128)S(1)}) all-reduce(f32[32,16]{0,1:T(8,128)S(1)} %convolution_bitcast_fusion.4, f32[32,32]{0,1:T(8,128)S(1)} %fusion.1), channel_id=1, replica_groups=mesh['rows'=16,'cols'=2] {'rows'}, use_global_device_ids=true, to_apply=%region_4.5 | all-reduce | flops 1536 | bytes 12288 | tf_op jit(solution)/shard_map/psum | solution.py:85
  76.7 2.9 %cholesky.16 = f32[32,32]{1,0:T(8,128)S(1)} custom-call(f32[32,32]{1,0:T(8,128)S(1)} %fusion.22), custom_call_target="Cholesky" | custom-call | tf_op jit(solution)/shard_map/jit(cholesky)/cholesky | solution.py:53
  81.0 2.4 %custom-call.10 = f32[1,32,32]{1,2,0:T(8,128)S(1)} custom-call(f32[1,32,32]{2,1,0:T(8,128)S(1)} %fusion.17), custom_call_target="InvertDiagBlocksLowerTriangular" | custom-call | tf_op jit(solution)/shard_map/jit(_cho_solve)/triangular_solve | solution.py:54
  87.7 3.5 %all-to-all-start.1 = ((f32[1,16,128]{2,0,1:T(1,128)}), f32[1,16,128]{2,0,1:T(1,128)S(1)}, u32[]{:S(2)}, u32[]{:S(2)}) async-start(f32[1,16,128]{2,0,1:T(1,128)} %bitcast.17), calls=%async_computation.1 | async-start | bytes 16384 | tf_op jit(solution)/shard_map/all_to_all | solution.py:98
  93.5 2.0 scatter_fusion
  95.4 2.1 all-to-all-done.1
  97.5 3.9 %all-to-all-start = ((f32[16,16,128]{2,0,1:T(8,128)}), f32[16,16,128]{2,0,1:T(8,128)S(1)}, u32[]{:S(2)}, u32[]{:S(2)}) async-start(f32[16,16,128]{2,0,1:T(8,128)} %scatter_fusion), calls=%async_computation | async-start | bytes 262144 | tf_op jit(solution)/shard_map/all_to_all | solution.py:91
  102.0 7.3 %all-to-all-done = f32[16,16,128]{2,0,1:T(8,128)S(1)} async-done(((f32[16,16,128]{2,0,1:T(8,128)}), f32[16,16,128]{2,0,1:T(8,128)S(1)}, u32[]{:S(2)}, u32[]{:S(2)}) %all-to-all-start) | async-done | bytes 131104 | tf_op jit(solution)/shard_map/all_to_all | solution.py:91
  119.1 2.4 %collective-permute-start.19 = (f32[16,1,128]{2,0,1:T(8,128)S(1)}, f32[16,1,128]{2,0,1:T(8,128)S(1)}, u32[]{:S(2)}, u32[]{:S(2)}) collective-permute-start(f32[16,1,128]{2,0,1:T(8,128)S(1)} %get-tuple-element.11), channel_id=1, source_target_pairs={{0,4},{2,6},{4,8},{6,10},{8,12},{10,14},{12,16},{14,18},{16,20},{1... | collective-permute-start | bytes 24584 | tf_op jit(solution)/shard_map/ppermute | solution.py:21
  121.5 2.2 collective-permute-start.18
  125.2 4.4 %collective-permute-start.7 = (f32[16,1,128]{2,0,1:T(8,128)S(1)}, f32[16,1,128]{2,0,1:T(8,128)S(1)}, u32[]{:S(2)}, u32[]{:S(2)}) collective-permute-start(f32[16,1,128]{2,0,1:T(8,128)S(1)} %get-tuple-element.23), channel_id=1, source_target_pairs={{0,28},{2,30},{4,0},{6,2},{8,4},{10,6},{12,8},{14,10},{16,12},{18,... | collective-permute-start | bytes 24584 | tf_op jit(solution)/shard_map/ppermute | solution.py:21
  131.1 3.1 %collective-permute-done.8 = f32[16,1,128]{2,0,1:T(8,128)S(1)} collective-permute-done((f32[16,1,128]{2,0,1:T(8,128)S(1)}, f32[16,1,128]{2,0,1:T(8,128)S(1)}, u32[]{:S(2)}, u32[]{:S(2)}) %collective-permute-start.8) | collective-permute-done | bytes 8224 | tf_op jit(solution)/shard_map/ppermute | solution.py:21
  135.3 2.5 %collective-permute-done.9 = f32[16,1,128]{2,0,1:T(8,128)S(1)} collective-permute-done((f32[16,1,128]{2,0,1:T(8,128)S(1)}, f32[16,1,128]{2,0,1:T(8,128)S(1)}, u32[]{:S(2)}, u32[]{:S(2)}) %collective-permute-start.9) | collective-permute-done | bytes 8224 | tf_op jit(solution)/shard_map/ppermute | solution.py:21
  137.8 2.4 %collective-permute-start.10 = (f32[16,1,128]{2,0,1:T(8,128)S(1)}, f32[16,1,128]{2,0,1:T(8,128)S(1)}, u32[]{:S(2)}, u32[]{:S(2)}) collective-permute-start(f32[16,1,128]{2,0,1:T(8,128)S(1)} %get-tuple-element.20), channel_id=1, source_target_pairs={{0,22},{2,24},{4,26},{6,28},{8,30},{10,0},{12,2},{14,4},{16,6},{18... | collective-permute-start | bytes 24584 | tf_op jit(solution)/shard_map/ppermute | solution.py:21
  141.5 5.6 %collective-permute-start.11 = (f32[16,1,128]{2,0,1:T(8,128)S(1)}, f32[16,1,128]{2,0,1:T(8,128)S(1)}, u32[]{:S(2)}, u32[]{:S(2)}) collective-permute-start(f32[16,1,128]{2,0,1:T(8,128)S(1)} %get-tuple-element.19), channel_id=1, source_target_pairs={{0,20},{2,22},{4,24},{6,26},{8,28},{10,30},{12,0},{14,2},{16,4},{1... | collective-permute-start | bytes 24584 | tf_op jit(solution)/shard_map/ppermute | solution.py:21
  148.4 3.8 %collective-permute-start.12 = (f32[16,1,128]{2,0,1:T(8,128)S(1)}, f32[16,1,128]{2,0,1:T(8,128)S(1)}, u32[]{:S(2)}, u32[]{:S(2)}) collective-permute-start(f32[16,1,128]{2,0,1:T(8,128)S(1)} %get-tuple-element.18), channel_id=1, source_target_pairs={{0,18},{2,20},{4,22},{6,24},{8,26},{10,28},{12,30},{14,0},{16,2},{... | collective-permute-start | bytes 24584 | tf_op jit(solution)/shard_map/ppermute | solution.py:21
  153.6 4.7 %collective-permute-start.13 = (f32[16,1,128]{2,0,1:T(8,128)S(1)}, f32[16,1,128]{2,0,1:T(8,128)S(1)}, u32[]{:S(2)}, u32[]{:S(2)}) collective-permute-start(f32[16,1,128]{2,0,1:T(8,128)S(1)} %get-tuple-element.17), channel_id=1, source_target_pairs={{0,16},{2,18},{4,20},{6,22},{8,24},{10,26},{12,28},{14,30},{16,0},... | collective-permute-start | bytes 24584 | tf_op jit(solution)/shard_map/ppermute | solution.py:21
  159.9 2.7 %collective-permute-start.14 = (f32[16,1,128]{2,0,1:T(8,128)S(1)}, f32[16,1,128]{2,0,1:T(8,128)S(1)}, u32[]{:S(2)}, u32[]{:S(2)}) collective-permute-start(f32[16,1,128]{2,0,1:T(8,128)S(1)} %get-tuple-element.16), channel_id=1, source_target_pairs={{0,14},{2,16},{4,18},{6,20},{8,22},{10,24},{12,26},{14,28},{16,30}... | collective-permute-start | bytes 24584 | tf_op jit(solution)/shard_map/ppermute | solution.py:21
  164.0 4.7 %collective-permute-start.15 = (f32[16,1,128]{2,0,1:T(8,128)S(1)}, f32[16,1,128]{2,0,1:T(8,128)S(1)}, u32[]{:S(2)}, u32[]{:S(2)}) collective-permute-start(f32[16,1,128]{2,0,1:T(8,128)S(1)} %get-tuple-element.15), channel_id=1, source_target_pairs={{0,12},{2,14},{4,16},{6,18},{8,20},{10,22},{12,24},{14,26},{16,28}... | collective-permute-start | bytes 24584 | tf_op jit(solution)/shard_map/ppermute | solution.py:21
  170.0 2.9 %collective-permute-start.16 = (f32[16,1,128]{2,0,1:T(8,128)S(1)}, f32[16,1,128]{2,0,1:T(8,128)S(1)}, u32[]{:S(2)}, u32[]{:S(2)}) collective-permute-start(f32[16,1,128]{2,0,1:T(8,128)S(1)} %get-tuple-element.14), channel_id=1, source_target_pairs={{0,10},{2,12},{4,14},{6,16},{8,18},{10,20},{12,22},{14,24},{16,26}... | collective-permute-start | bytes 24584 | tf_op jit(solution)/shard_map/ppermute | solution.py:21
  178.2 4.9 %collective-permute-done.22 = f32[16,512]{1,0:T(8,128)S(1)} collective-permute-done((f32[16,512]{1,0:T(8,128)S(1)}, f32[16,512]{1,0:T(8,128)S(1)}, u32[]{:S(2)}, u32[]{:S(2)}) %collective-permute-start.22) | collective-permute-done | bytes 32800 | tf_op jit(solution)/shard_map/ppermute | solution.py:38
  184.9 32.1 %psum.23 = f32[16]{0:T(128)S(1)} all-reduce(f32[16]{0:T(128)S(1)} %get-tuple-element.8), channel_id=1, replica_groups=mesh['rows'=16,'cols'=2] {'rows'}, use_global_device_ids=true, to_apply=%region_9.11 | all-reduce | flops 16 | bytes 128 | tf_op jit(solution)/shard_map/psum | solution.py:115
  (105 shorter events, 44.7 us)
Async XLA Ops:
  0.8 11.8 %collective-permute-start = (f32[16,512]{1,0:T(8,128)S(1)}, f32[16,512]{1,0:T(8,128)S(1)}, u32[]{:S(2)}, u32[]{:S(2)}) collective-permute-start(f32[16,512]{1,0:T(8,128)S(1)} %get-tuple-element.31), channel_id=1, source_target_pairs={{0,2},{2,4},{4,6},{6,8},{8,10},{10,12},{12,14},{14,16},{16,18},{18... | collective-permute-start | bytes 98312 | tf_op jit(solution)/shard_map/ppermute | solution.py:37
  3.2 9.4 %collective-permute-start.1 = (f32[16,512]{1,0:T(8,128)S(1)}, f32[16,512]{1,0:T(8,128)S(1)}, u32[]{:S(2)}, u32[]{:S(2)}) collective-permute-start(f32[16,512]{1,0:T(8,128)S(1)} %get-tuple-element.32), channel_id=1, source_target_pairs={{2,0},{4,2},{6,4},{8,6},{10,8},{12,10},{14,12},{16,14},{18,16},{20... | collective-permute-start | bytes 98312 | tf_op jit(solution)/shard_map/ppermute | solution.py:38
  83.9 7.3 %collective-permute-start.2 = (f32[16,512]{1,0:T(8,128)S(1)}, f32[16,512]{1,0:T(8,128)S(1)}, u32[]{:S(2)}, u32[]{:S(2)}) collective-permute-start(f32[16,512]{1,0:T(8,128)S(1)} %get-tuple-element.29), channel_id=1, source_target_pairs={{0,2},{2,4},{4,6},{6,8},{8,10},{10,12},{12,14},{14,16},{16,18},{18... | collective-permute-start | bytes 98312 | tf_op jit(solution)/shard_map/ppermute | solution.py:37
  85.2 6.0 %collective-permute-start.3 = (f32[16,512]{1,0:T(8,128)S(1)}, f32[16,512]{1,0:T(8,128)S(1)}, u32[]{:S(2)}, u32[]{:S(2)}) collective-permute-start(f32[16,512]{1,0:T(8,128)S(1)} %get-tuple-element.30), channel_id=1, source_target_pairs={{2,0},{4,2},{6,4},{8,6},{10,8},{12,10},{14,12},{16,14},{18,16},{20... | collective-permute-start | bytes 98312 | tf_op jit(solution)/shard_map/ppermute | solution.py:38
  87.7 9.8 %all-to-all-start.1 = ((f32[1,16,128]{2,0,1:T(1,128)}), f32[1,16,128]{2,0,1:T(1,128)S(1)}, u32[]{:S(2)}, u32[]{:S(2)}) async-start(f32[1,16,128]{2,0,1:T(1,128)} %bitcast.17), calls=%async_computation.1 | async-start | bytes 16384 | tf_op jit(solution)/shard_map/all_to_all | solution.py:98
  97.5 11.8 %all-to-all-start = ((f32[16,16,128]{2,0,1:T(8,128)}), f32[16,16,128]{2,0,1:T(8,128)S(1)}, u32[]{:S(2)}, u32[]{:S(2)}) async-start(f32[16,16,128]{2,0,1:T(8,128)} %scatter_fusion), calls=%async_computation | async-start | bytes 262144 | tf_op jit(solution)/shard_map/all_to_all | solution.py:91
  109.9 2.6 %collective-permute-start.4 = (f32[16,512]{1,0:T(8,128)S(1)}, f32[16,512]{1,0:T(8,128)S(1)}, u32[]{:S(2)}, u32[]{:S(2)}) collective-permute-start(f32[16,512]{1,0:T(8,128)S(1)} %get-tuple-element.27), channel_id=1, source_target_pairs={{0,2},{2,4},{4,6},{6,8},{8,10},{10,12},{12,14},{14,16},{16,18},{18... | collective-permute-start | bytes 98312 | tf_op jit(solution)/shard_map/ppermute | solution.py:37
  111.2 3.1 %collective-permute-start.5 = (f32[16,512]{1,0:T(8,128)S(1)}, f32[16,512]{1,0:T(8,128)S(1)}, u32[]{:S(2)}, u32[]{:S(2)}) collective-permute-start(f32[16,512]{1,0:T(8,128)S(1)} %get-tuple-element.28), channel_id=1, source_target_pairs={{2,0},{4,2},{6,4},{8,6},{10,8},{12,10},{14,12},{16,14},{18,16},{20... | collective-permute-start | bytes 98312 | tf_op jit(solution)/shard_map/ppermute | solution.py:38
  116.7 8.5 %collective-permute-start.6 = (f32[16,1,128]{2,0,1:T(8,128)S(1)}, f32[16,1,128]{2,0,1:T(8,128)S(1)}, u32[]{:S(2)}, u32[]{:S(2)}) collective-permute-start(f32[16,1,128]{2,0,1:T(8,128)S(1)} %get-tuple-element.24), channel_id=1, source_target_pairs={{0,30},{2,0},{4,2},{6,4},{8,6},{10,8},{12,10},{14,12},{16,14},{18,... | collective-permute-start | bytes 24584 | tf_op jit(solution)/shard_map/ppermute | solution.py:21
  118.4 56.6 %collective-permute-start.20 = (f32[16,1,128]{2,0,1:T(8,128)S(1)}, f32[16,1,128]{2,0,1:T(8,128)S(1)}, u32[]{:S(2)}, u32[]{:S(2)}) collective-permute-start(f32[16,1,128]{2,0,1:T(8,128)S(1)} %get-tuple-element.10), channel_id=1, source_target_pairs={{0,2},{2,4},{4,6},{6,8},{8,10},{10,12},{12,14},{14,16},{16,18},{18... | collective-permute-start | bytes 24584 | tf_op jit(solution)/shard_map/ppermute | solution.py:21
  119.1 55.8 %collective-permute-start.19 = (f32[16,1,128]{2,0,1:T(8,128)S(1)}, f32[16,1,128]{2,0,1:T(8,128)S(1)}, u32[]{:S(2)}, u32[]{:S(2)}) collective-permute-start(f32[16,1,128]{2,0,1:T(8,128)S(1)} %get-tuple-element.11), channel_id=1, source_target_pairs={{0,4},{2,6},{4,8},{6,10},{8,12},{10,14},{12,16},{14,18},{16,20},{1... | collective-permute-start | bytes 24584 | tf_op jit(solution)/shard_map/ppermute | solution.py:21
  121.5 53.4 %collective-permute-start.18 = (f32[16,1,128]{2,0,1:T(8,128)S(1)}, f32[16,1,128]{2,0,1:T(8,128)S(1)}, u32[]{:S(2)}, u32[]{:S(2)}) collective-permute-start(f32[16,1,128]{2,0,1:T(8,128)S(1)} %get-tuple-element.12), channel_id=1, source_target_pairs={{0,6},{2,8},{4,10},{6,12},{8,14},{10,16},{12,18},{14,20},{16,22},{... | collective-permute-start | bytes 24584 | tf_op jit(solution)/shard_map/ppermute | solution.py:21
  123.6 51.2 %collective-permute-start.17 = (f32[16,1,128]{2,0,1:T(8,128)S(1)}, f32[16,1,128]{2,0,1:T(8,128)S(1)}, u32[]{:S(2)}, u32[]{:S(2)}) collective-permute-start(f32[16,1,128]{2,0,1:T(8,128)S(1)} %get-tuple-element.13), channel_id=1, source_target_pairs={{0,8},{2,10},{4,12},{6,14},{8,16},{10,18},{12,20},{14,22},{16,24},... | collective-permute-start | bytes 24584 | tf_op jit(solution)/shard_map/ppermute | solution.py:21
  125.2 5.8 %collective-permute-start.7 = (f32[16,1,128]{2,0,1:T(8,128)S(1)}, f32[16,1,128]{2,0,1:T(8,128)S(1)}, u32[]{:S(2)}, u32[]{:S(2)}) collective-permute-start(f32[16,1,128]{2,0,1:T(8,128)S(1)} %get-tuple-element.23), channel_id=1, source_target_pairs={{0,28},{2,30},{4,0},{6,2},{8,4},{10,6},{12,8},{14,10},{16,12},{18,... | collective-permute-start | bytes 24584 | tf_op jit(solution)/shard_map/ppermute | solution.py:21
  131.1 3.1 %collective-permute-start.8 = (f32[16,1,128]{2,0,1:T(8,128)S(1)}, f32[16,1,128]{2,0,1:T(8,128)S(1)}, u32[]{:S(2)}, u32[]{:S(2)}) collective-permute-start(f32[16,1,128]{2,0,1:T(8,128)S(1)} %get-tuple-element.22), channel_id=1, source_target_pairs={{0,26},{2,28},{4,30},{6,0},{8,2},{10,4},{12,6},{14,8},{16,10},{18,... | collective-permute-start | bytes 24584 | tf_op jit(solution)/shard_map/ppermute | solution.py:21
  134.1 3.7 %collective-permute-start.9 = (f32[16,1,128]{2,0,1:T(8,128)S(1)}, f32[16,1,128]{2,0,1:T(8,128)S(1)}, u32[]{:S(2)}, u32[]{:S(2)}) collective-permute-start(f32[16,1,128]{2,0,1:T(8,128)S(1)} %get-tuple-element.21), channel_id=1, source_target_pairs={{0,24},{2,26},{4,28},{6,30},{8,0},{10,2},{12,4},{14,6},{16,8},{18,... | collective-permute-start | bytes 24584 | tf_op jit(solution)/shard_map/ppermute | solution.py:21
  137.8 3.7 %collective-permute-start.10 = (f32[16,1,128]{2,0,1:T(8,128)S(1)}, f32[16,1,128]{2,0,1:T(8,128)S(1)}, u32[]{:S(2)}, u32[]{:S(2)}) collective-permute-start(f32[16,1,128]{2,0,1:T(8,128)S(1)} %get-tuple-element.20), channel_id=1, source_target_pairs={{0,22},{2,24},{4,26},{6,28},{8,30},{10,0},{12,2},{14,4},{16,6},{18... | collective-permute-start | bytes 24584 | tf_op jit(solution)/shard_map/ppermute | solution.py:21
  141.5 6.9 %collective-permute-start.11 = (f32[16,1,128]{2,0,1:T(8,128)S(1)}, f32[16,1,128]{2,0,1:T(8,128)S(1)}, u32[]{:S(2)}, u32[]{:S(2)}) collective-permute-start(f32[16,1,128]{2,0,1:T(8,128)S(1)} %get-tuple-element.19), channel_id=1, source_target_pairs={{0,20},{2,22},{4,24},{6,26},{8,28},{10,30},{12,0},{14,2},{16,4},{1... | collective-permute-start | bytes 24584 | tf_op jit(solution)/shard_map/ppermute | solution.py:21
  148.4 5.2 %collective-permute-start.12 = (f32[16,1,128]{2,0,1:T(8,128)S(1)}, f32[16,1,128]{2,0,1:T(8,128)S(1)}, u32[]{:S(2)}, u32[]{:S(2)}) collective-permute-start(f32[16,1,128]{2,0,1:T(8,128)S(1)} %get-tuple-element.18), channel_id=1, source_target_pairs={{0,18},{2,20},{4,22},{6,24},{8,26},{10,28},{12,30},{14,0},{16,2},{... | collective-permute-start | bytes 24584 | tf_op jit(solution)/shard_map/ppermute | solution.py:21
  153.6 6.3 %collective-permute-start.13 = (f32[16,1,128]{2,0,1:T(8,128)S(1)}, f32[16,1,128]{2,0,1:T(8,128)S(1)}, u32[]{:S(2)}, u32[]{:S(2)}) collective-permute-start(f32[16,1,128]{2,0,1:T(8,128)S(1)} %get-tuple-element.17), channel_id=1, source_target_pairs={{0,16},{2,18},{4,20},{6,22},{8,24},{10,26},{12,28},{14,30},{16,0},... | collective-permute-start | bytes 24584 | tf_op jit(solution)/shard_map/ppermute | solution.py:21
  159.9 4.0 %collective-permute-start.14 = (f32[16,1,128]{2,0,1:T(8,128)S(1)}, f32[16,1,128]{2,0,1:T(8,128)S(1)}, u32[]{:S(2)}, u32[]{:S(2)}) collective-permute-start(f32[16,1,128]{2,0,1:T(8,128)S(1)} %get-tuple-element.16), channel_id=1, source_target_pairs={{0,14},{2,16},{4,18},{6,20},{8,22},{10,24},{12,26},{14,28},{16,30}... | collective-permute-start | bytes 24584 | tf_op jit(solution)/shard_map/ppermute | solution.py:21
  164.0 6.0 %collective-permute-start.15 = (f32[16,1,128]{2,0,1:T(8,128)S(1)}, f32[16,1,128]{2,0,1:T(8,128)S(1)}, u32[]{:S(2)}, u32[]{:S(2)}) collective-permute-start(f32[16,1,128]{2,0,1:T(8,128)S(1)} %get-tuple-element.15), channel_id=1, source_target_pairs={{0,12},{2,14},{4,16},{6,18},{8,20},{10,22},{12,24},{14,26},{16,28}... | collective-permute-start | bytes 24584 | tf_op jit(solution)/shard_map/ppermute | solution.py:21
  170.0 4.9 %collective-permute-start.16 = (f32[16,1,128]{2,0,1:T(8,128)S(1)}, f32[16,1,128]{2,0,1:T(8,128)S(1)}, u32[]{:S(2)}, u32[]{:S(2)}) collective-permute-start(f32[16,1,128]{2,0,1:T(8,128)S(1)} %get-tuple-element.14), channel_id=1, source_target_pairs={{0,10},{2,12},{4,14},{6,16},{8,18},{10,20},{12,22},{14,24},{16,26}... | collective-permute-start | bytes 24584 | tf_op jit(solution)/shard_map/ppermute | solution.py:21
  176.9 6.3 %collective-permute-start.22 = (f32[16,512]{1,0:T(8,128)S(1)}, f32[16,512]{1,0:T(8,128)S(1)}, u32[]{:S(2)}, u32[]{:S(2)}) collective-permute-start(f32[16,512]{1,0:T(8,128)S(1)} %get-tuple-element.26), channel_id=1, source_target_pairs={{2,0},{4,2},{6,4},{8,6},{10,8},{12,10},{14,12},{16,14},{18,16},{20... | collective-permute-start | bytes 98312 | tf_op jit(solution)/shard_map/ppermute | solution.py:38
  (4 other events, 89.9 us)
